TPU v7x, 256 devices: a whole 4x4x8 slice. The times are simulated.
256 devices in a mesh: pool: 16 (over z, core), tensor: 16 (over y, x).
Axes of the slice: x: 4, y: 4, z: 8, core: 2. Of those that a mesh axis runs over, the one named last changes fastest.
Arguments:
- hidden: bfloat16 [8192, 14336], P('pool', 'tensor'), may hold values from -6 to 6
- down_weight: bfloat16 [14336, 8192], P('tensor', 'pool'), may hold values from -0.046875 to 0.046875
- adapter_shrink: bfloat16 [32, 14336, 64], P('pool', 'tensor'), may hold values from -0.046875 to 0.046875
- adapter_expand: bfloat16 [32, 8192, 64], P('pool', 'tensor'), may hold values from -0.75 to 0.75
- block_adapter: int32 [64], P('pool'), may hold values from 0 to 31, as said below
- block_rows: int32 [64], P('pool'), may hold values from 1 to 128, 6144 in all
Outputs:
- projected: bfloat16 [8192, 8192], P(('pool', 'tensor'))
Inputs may be any that keep to these rules, and one draw needn't show every extreme that they name: `block_adapter`: within each aligned run of 4 blocks (the rows of one pool index) no two blocks name adapters with the same a // 2. `block_rows`: some block is full.
All inputs are finite; a program needn't handle non-finite values.
Results may differ from a plain program's by a relative error of at most 0.02.
Values may be sent and summed in bfloat16 or wider, within the bound.
A program may use at most 128 MiB of HBM per device.

v0:
```python
import jax
import jax.numpy as jnp
from jax import lax
from jax.sharding import PartitionSpec as P

BLOCK = 128
adapter_scale_factor = 0.5


def shards(hidden, down_weight, adapter_shrink, adapter_expand, block_adapter, block_rows):
    input_rows, feat = hidden.shape
    block_count = block_adapter.shape[0]
    column_span = adapter_expand.shape[1]
    tensor_pos = lax.axis_index("tensor")
    tensor_count = lax.axis_size("tensor")
    own_rows = input_rows // tensor_count
    blocks = hidden.reshape(block_count, BLOCK, feat)
    partial_value = jnp.dot(
        hidden,
        lax.all_gather(down_weight, "pool", axis=1, tiled=True),
        preferred_element_type=jnp.float32,
    )
    total = lax.psum_scatter(
        partial_value.astype(jnp.bfloat16), "tensor", scatter_dimension=0, tiled=True
    ).astype(jnp.float32)
    shrink_piece = lax.all_gather(adapter_shrink, "pool", axis=0, tiled=True)
    expand_piece = lax.all_gather(adapter_expand, "pool", axis=0, tiled=True)
    idents = jnp.arange(shrink_piece.shape[0], dtype=jnp.int32)
    pick = (block_adapter[:, None] == idents[None, :]).astype(jnp.bfloat16)
    first = jnp.einsum("bk,kfr->bfr", pick, shrink_piece, preferred_element_type=jnp.float32)
    second = jnp.einsum("bk,kcr->bcr", pick, expand_piece, preferred_element_type=jnp.float32)
    shrink = jnp.einsum(
        "bnf,bfr->bnr", blocks, first.astype(jnp.bfloat16), preferred_element_type=jnp.float32
    )
    summed_shrink = lax.psum(shrink.astype(jnp.bfloat16), "tensor")
    enlarged_rows = jnp.einsum(
        "bnr,bcr->bnc",
        summed_shrink,
        second.astype(jnp.bfloat16),
        preferred_element_type=jnp.float32,
    )
    adapter_delta_columns = (
        (adapter_scale_factor * enlarged_rows).astype(jnp.bfloat16).reshape(input_rows, column_span)
    )
    delta_mine = lax.all_to_all(
        adapter_delta_columns, "tensor", split_axis=0, concat_axis=1, tiled=True
    )
    total = total + delta_mine.astype(jnp.float32)
    row_ids = tensor_pos * own_rows + jnp.arange(own_rows, dtype=jnp.int32)
    owning = (row_ids // BLOCK)[:, None] == jnp.arange(block_count, dtype=jnp.int32)[None, :]
    lengths = jnp.sum(jnp.where(owning, block_rows[None, :], 0), axis=1)
    valid = (row_ids % BLOCK < lengths).astype(jnp.float32)
    return (total * valid[:, None]).astype(jnp.bfloat16)


def solution(mesh):
    in_specs = (
        P("pool", "tensor"),
        P("tensor", "pool"),
        P("pool", "tensor", None),
        P("pool", "tensor", None),
        P("pool"),
        P("pool"),
    )
    out_specs = P(("pool", "tensor"), None)
    return jax.shard_map(shards, mesh=mesh, in_specs=in_specs, out_specs=out_specs, check_vma=False)
```

profile of v0, /device:TPU:2, one launch (start us, length us, event | category | flops | bytes accessed | tf_op | source)
XLA Modules:
  0.0 374.3 jit_solution(14904361085306204502)
XLA Ops:
  6.5 0.7 all-gather.6.cloned.1.call-update
  7.3 0.0 all-gather.4.cloned.1.call-start
  7.3 0.7 all-gather.4.cloned.1.call-update
  8.0 0.0 all-gather.8.cloned.1.call-start
  8.1 0.7 all-gather.8.cloned.1.call-update
  8.7 0.0 all-reduce.2.cloned.1.call-start
  8.8 45.0 %all-gather.6.cloned.1.call-done = bf16[32,896,64]{1,2,0:T(8,128)(2,1)} async-done(((bf16[2,896,64]{1,2,0:T(8,128)(2,1)}), bf16[32,896,64]{1,2,0:T(8,128)(2,1)}) %all-gather.6.cloned.1.call-update) | async-done | bytes 3670032 | tf_op jit(solution)/shard_map/all_gather | solution.py:26
  53.8 5.0 %fusion.5 = bf16[4,896,64]{1,0,2:T(4,128)(2,1)S(1)} fusion(bf16[32,896,64]{1,2,0:T(8,128)(2,1)} %all-gather.6.cloned.1.call-done, s32[4]{0:T(128)} %param.10), kind=kOutput, calls=%fused_computation.7 | convolution fusion | flops 14909568 | bytes 4128784 | tf_op jit(solution)/shard_map/bk,kfr->bfr/dot_general | solution.py:30
  58.8 1.1 fusion.11
  59.9 0.0 reduce-scatter.2.cloned.1.call-start
  59.9 79.8 %all-gather.4.cloned.1.call-done = bf16[896,8192]{1,0:T(8,128)(2,1)} async-done(((bf16[896,512]{1,0:T(8,128)(2,1)}), bf16[896,8192]{1,0:T(8,128)(2,1)}) %all-gather.4.cloned.1.call-update) | async-done | bytes 14680080 | tf_op jit(solution)/shard_map/all_gather | solution.py:20
  139.8 16.5 %convolution_convert_fusion = bf16[512,8192]{1,0:T(8,128)(2,1)} fusion(bf16[512,896]{1,0:T(8,128)(2,1)S(1)} %copy-done, bf16[896,8192]{1,0:T(8,128)(2,1)} %all-gather.4.cloned.1.call-done), kind=kOutput, calls=%fused_computation | convolution fusion | flops 7520387072 | bytes 23986176 | tf_op jit(solution)/shard_map/dot_general | solution.py:18
  156.3 0.0 reduce-scatter.2.cloned.1.call-update
  156.3 23.6 %all-gather.8.cloned.1.call-done = bf16[32,512,64]{1,2,0:T(8,128)(2,1)} async-done(((bf16[2,512,64]{1,2,0:T(8,128)(2,1)}), bf16[32,512,64]{1,2,0:T(8,128)(2,1)}) %all-gather.8.cloned.1.call-update) | async-done | bytes 2097168 | tf_op jit(solution)/shard_map/all_gather | solution.py:27
  179.9 2.9 fusion.8
  182.8 89.2 %all-reduce.2.cloned.1.call-done = bf16[4,128,64]{1,2,0:T(8,128)(2,1)} async-done(((bf16[4,128,64]{1,2,0:T(8,128)(2,1)}), bf16[4,128,64]{1,2,0:T(8,128)(2,1)}) %all-reduce.2.cloned.1.call-update) | async-done | bytes 65552 | tf_op jit(solution)/shard_map/psum | solution.py:35
  272.0 2.0 fusion.4
  274.0 5.7 %all-to-all-start = ((bf16[16,32,512]{2,1,0:T(8,128)(2,1)}), bf16[16,32,512]{2,1,0:T(8,128)(2,1)S(1)}, u32[]{:S(2)}, u32[]{:S(2)}) async-start(bf16[16,32,512]{2,1,0:T(8,128)(2,1)} %bitcast.3), calls=%async_computation.1 | async-start | bytes 1048576 | tf_op jit(solution)/shard_map/all_to_all | solution.py:45
  279.8 0.1 select_reduce_fusion
  279.9 8.6 %all-to-all-done = bf16[16,32,512]{2,1,0:T(8,128)(2,1)S(1)} async-done(((bf16[16,32,512]{2,1,0:T(8,128)(2,1)}), bf16[16,32,512]{2,1,0:T(8,128)(2,1)S(1)}, u32[]{:S(2)}, u32[]{:S(2)}) %all-to-all-start) | async-done | bytes 524320 | tf_op jit(solution)/shard_map/all_to_all | solution.py:45
  288.5 0.1 convert_bitcast_fusion
  288.6 0.1 copy.14
  288.7 77.0 %reduce-scatter.2.cloned.1.call-done = bf16[32,8192]{1,0:T(8,128)(2,1)} async-done(((bf16[512,8192]{1,0:T(8,128)(2,1)}), bf16[32,8192]{1,0:T(8,128)(2,1)}) %reduce-scatter.2.cloned.1.call-update) | async-done | bytes 524304 | tf_op jit(solution)/shard_map/reduce_scatter | solution.py:23
  365.7 2.0 multiply_convert_fusion
  (10 shorter events, 0.1 us)
Async XLA Ops:
  6.5 52.2 %copy-start = (bf16[512,896]{1,0:T(8,128)(2,1)S(1)}, bf16[512,896]{1,0:T(8,128)(2,1)}, u32[]{:S(2)}) copy-start(bf16[512,896]{1,0:T(8,128)(2,1)} %param.6) | copy-start | bytes 2752516
  6.5 47.2 %all-gather.6.cloned.1.call-start = ((), (), s32[]{:S(2)}) async-start(), calls=%async_computation.4 | async-start | bytes 3899392 | tf_op jit(solution)/shard_map/all_gather | solution.py:26
  7.3 132.5 %all-gather.4.cloned.1.call-start = ((), (), s32[]{:S(2)}) async-start(), calls=%async_computation.2 | async-start | bytes 15597568 | tf_op jit(solution)/shard_map/all_gather | solution.py:20
  8.0 171.9 %all-gather.8.cloned.1.call-start = ((), (), s32[]{:S(2)}) async-start(), calls=%async_computation.6 | async-start | bytes 2228224 | tf_op jit(solution)/shard_map/all_gather | solution.py:27
  8.7 263.3 %all-reduce.2.cloned.1.call-start = ((), (), s32[]{:S(2)}) async-start(), calls=%async_computation.5 | async-start | bytes 131072 | tf_op jit(solution)/shard_map/psum | solution.py:35
  59.9 305.8 %reduce-scatter.2.cloned.1.call-start = ((), (), s32[]{:S(2)}) async-start(), calls=%async_computation.3 | async-start | bytes 8912896 | tf_op jit(solution)/shard_map/reduce_scatter | solution.py:23
  156.3 23.6 %copy-start.1 = (s32[4]{0:T(128)S(1)}, s32[4]{0:T(128)}, u32[]{:S(2)}) copy-start(s32[4]{0:T(128)} %param.10) | copy-start | bytes 52
  156.3 123.4 %copy-start.2 = (s32[4]{0:T(128)S(1)}, s32[4]{0:T(128)}, u32[]{:S(2)}) copy-start(s32[4]{0:T(128)} %param.11) | copy-start | bytes 52
  274.0 14.5 %all-to-all-start = ((bf16[16,32,512]{2,1,0:T(8,128)(2,1)}), bf16[16,32,512]{2,1,0:T(8,128)(2,1)S(1)}, u32[]{:S(2)}, u32[]{:S(2)}) async-start(bf16[16,32,512]{2,1,0:T(8,128)(2,1)} %bitcast.3), calls=%async_computation.1 | async-start | bytes 1048576 | tf_op jit(solution)/shard_map/all_to_all | solution.py:45
Sparse Core Ops, SparseCore 0:
  9.2 44.5 all-gather.5
  55.6 84.1 all-gather.3
  141.6 38.2 all-gather.7
  183.0 89.0 all-reduce.1
  276.0 89.6 reduce-scatter.1
where the time goes:
time: 375 us; the launch traced here: 374 us
  waiting for transfers between devices  325 us (87%)
  matrix products  27.4 us (7%)
  between operations  13.2 us (4%)
  starting transfers between devices  5.89 us (2%)
    psum x1, waiting for transfers between devices, shards(): summed_shrink = lax.psum(shrink.astype(jnp.bfloat16), 'tensor')  89.2 us
    all_gather x1, waiting for transfers between devices, shards(): lax.all_gather(down_weight, 'pool', axis=1, tiled=True)  79.8 us
    reduce_scatter x1, waiting for transfers between devices, shards(): lax.psum_scatter(partial_value.astype(jnp.bfloat16), 'tensor', scatter_di...  77 us
    all_gather x1, waiting for transfers between devices, shards(): shrink_piece = lax.all_gather(adapter_shrink, 'pool', axis=0, tiled=True)  45 us
    all_gather x1, waiting for transfers between devices, shards(): expand_piece = lax.all_gather(adapter_expand, 'pool', axis=0, tiled=True)  23.6 us
    dot_general x1, matrix products, shards(): jnp.dot(hidden, lax.all_gather(down_weight, 'pool', axis=1, tiled=True),...  16.5 us
    all_to_all x1, waiting for transfers between devices, shards(): lax.all_to_all(adapter_delta_columns, 'tensor', split_axis=0, concat_axis...  8.61 us
  transfers between devices with their start and end apart: 6, of which 6 were waited for; matrix products, arithmetic and copies ran while one was open for 7% of the time, Pallas kernels for 0%

commit v1 on v0

--- a/solution.py
+++ b/solution.py
@@ -5,6 +5,18 @@
 
 BLOCK = 128
 adapter_scale_factor = 0.5
+
+
+def summed_around(x, axis, dim, product):
+    devices, mine, extent = (lax.axis_size(axis), lax.axis_index(axis), x.shape[dim])
+    right = [(i, (i + 1) % devices) for i in range(devices)]
+    held, total = (x, None)
+    for hop in range(devices):
+        coming = lax.ppermute(held, axis, right) if hop < devices - 1 else None
+        absorb = product(held, (mine - hop) % devices * extent)
+        total = absorb if total is None else total + absorb
+        held = coming
+    return total
 
 
 def shards(hidden, down_weight, adapter_shrink, adapter_expand, block_adapter, block_rows):
@@ -24,11 +36,20 @@
         partial_value.astype(jnp.bfloat16), "tensor", scatter_dimension=0, tiled=True
     ).astype(jnp.float32)
     shrink_piece = lax.all_gather(adapter_shrink, "pool", axis=0, tiled=True)
-    expand_piece = lax.all_gather(adapter_expand, "pool", axis=0, tiled=True)
     idents = jnp.arange(shrink_piece.shape[0], dtype=jnp.int32)
     pick = (block_adapter[:, None] == idents[None, :]).astype(jnp.bfloat16)
     first = jnp.einsum("bk,kfr->bfr", pick, shrink_piece, preferred_element_type=jnp.float32)
-    second = jnp.einsum("bk,kcr->bcr", pick, expand_piece, preferred_element_type=jnp.float32)
+    second = summed_around(
+        adapter_expand,
+        "pool",
+        0,
+        lambda part, at: jnp.einsum(
+            "bk,kcr->bcr",
+            lax.dynamic_slice_in_dim(pick, at, part.shape[0], axis=1),
+            part,
+            preferred_element_type=jnp.float32,
+        ),
+    )
     shrink = jnp.einsum(
         "bnf,bfr->bnr", blocks, first.astype(jnp.bfloat16), preferred_element_type=jnp.float32
     )

time: 375 us -> 336 us (0.90)
  waiting for transfers between devices: 325 us -> 281 us
    psum x1, waiting for transfers between devices: 89.2 us -> 0.02 us  [shards(): summed_shrink = lax.psum(shrink.astype(jnp.bfloat16), 'tensor')]
    ppermute x0 -> x15, waiting for transfers between devices: none -> 78.2 us  [summed_around(): coming = lax.ppermute(held, axis, right) if hop < devices - 1 else None]
    all_gather x1 -> x0, waiting for transfers between devices: 23.6 us -> none  [shards(): expand_piece = lax.all_gather(adapter_expand, 'pool', axis=0, tiled=True)]
    reduce_scatter x1, waiting for transfers between devices: 77 us -> 63.7 us  [shards(): lax.psum_scatter(partial_value.astype(jnp.bfloat16), 'tensor', scatter_di...]
  transfers between devices with their start and end apart: 6 -> 20, of which waited for: 6 -> 19; matrix products, arithmetic and copies ran while one was open for 7% -> 9% of each run, Pallas kernels for 0% -> 0%
where the time goes in v1:
time: 336 us
  waiting for transfers between devices  281 us (84%)
  matrix products  30.2 us (9%)
  between operations  13.4 us (4%)
  starting transfers between devices  7.89 us (2%)
    all_gather x1, waiting for transfers between devices, shards(): lax.all_gather(down_weight, 'pool', axis=1, tiled=True)  79.7 us
    ppermute x15, waiting for transfers between devices, summed_around(): coming = lax.ppermute(held, axis, right) if hop < devices - 1 else None  78.2 us
    reduce_scatter x1, waiting for transfers between devices, shards(): lax.psum_scatter(partial_value.astype(jnp.bfloat16), 'tensor', scatter_di...  63.7 us
    all_gather x1, waiting for transfers between devices, shards(): shrink_piece = lax.all_gather(adapter_shrink, 'pool', axis=0, tiled=True)  45.7 us
    dot_general x1, matrix products, shards(): jnp.dot(hidden, lax.all_gather(down_weight, 'pool', axis=1, tiled=True),...  16.5 us
    all_to_all x1, waiting for transfers between devices, shards(): lax.all_to_all(adapter_delta_columns, 'tensor', split_axis=0, concat_axis...  12.2 us
    all_to_all x1, starting transfers between devices, shards(): lax.all_to_all(adapter_delta_columns, 'tensor', split_axis=0, concat_axis...  7.28 us
  transfers between devices with their start and end apart: 20, of which 19 were waited for; matrix products, arithmetic and copies ran while one was open for 9% of the time, Pallas kernels for 0%

profile of v1, /device:TPU:2, one launch (start us, length us, event | category | flops | bytes accessed | tf_op | source)
XLA Modules:
  0.0 335.7 jit_solution(7685385895043934131)
XLA Ops:
  8.1 45.7 %all-gather.5.cloned.1.call-done = bf16[32,896,64]{1,2,0:T(8,128)(2,1)} async-done(((bf16[2,896,64]{1,2,0:T(8,128)(2,1)}), bf16[32,896,64]{1,2,0:T(8,128)(2,1)}) %all-gather.5.cloned.1.call-update) | async-done | bytes 3670032 | tf_op jit(solution)/shard_map/all_gather | solution.py:38
  53.8 5.0 %fusion.3 = bf16[4,896,64]{1,0,2:T(4,128)(2,1)S(1)} fusion(bf16[32,896,64]{1,2,0:T(8,128)(2,1)} %all-gather.5.cloned.1.call-done, s32[4]{0:T(128)} %param.10), kind=kOutput, calls=%fused_computation.5 | convolution fusion | flops 14909568 | bytes 4128784 | tf_op jit(solution)/shard_map/bk,kfr->bfr/dot_general | solution.py:41
  60.1 79.7 %all-gather.3.cloned.1.call-done = bf16[896,8192]{1,0:T(8,128)(2,1)} async-done(((bf16[896,512]{1,0:T(8,128)(2,1)}), bf16[896,8192]{1,0:T(8,128)(2,1)}) %all-gather.3.cloned.1.call-update) | async-done | bytes 14680080 | tf_op jit(solution)/shard_map/all_gather | solution.py:32
  139.8 16.5 %convolution_convert_fusion = bf16[512,8192]{1,0:T(8,128)(2,1)} fusion(bf16[512,896]{1,0:T(8,128)(2,1)S(1)} %copy-done, bf16[896,8192]{1,0:T(8,128)(2,1)} %all-gather.3.cloned.1.call-done), kind=kOutput, calls=%fused_computation | convolution fusion | flops 7520387072 | bytes 23986176 | tf_op jit(solution)/shard_map/dot_general | solution.py:30
  158.0 4.9 %collective-permute-done = bf16[2,512,64]{1,0,2:T(2,128)(2,1)S(1)} collective-permute-done((bf16[2,512,64]{1,0,2:T(2,128)(2,1)S(1)}, bf16[2,512,64]{1,0,2:T(2,128)(2,1)S(1)}, u32[]{:S(2)}, u32[]{:S(2)}) %collective-permute-start) | collective-permute-done | bytes 131104 | tf_op jit(solution)/shard_map/ppermute | solution.py:15
  163.3 5.2 %collective-permute-done.1 = bf16[2,512,64]{1,0,2:T(2,128)(2,1)S(1)} collective-permute-done((bf16[2,512,64]{1,0,2:T(2,128)(2,1)S(1)}, bf16[2,512,64]{1,0,2:T(2,128)(2,1)S(1)}, u32[]{:S(2)}, u32[]{:S(2)}) %collective-permute-start.1) | collective-permute-done | bytes 131104 | tf_op jit(solution)/shard_map/ppermute | solution.py:15
  168.9 5.2 %collective-permute-done.2 = bf16[2,512,64]{1,0,2:T(2,128)(2,1)S(1)} collective-permute-done((bf16[2,512,64]{1,0,2:T(2,128)(2,1)S(1)}, bf16[2,512,64]{1,0,2:T(2,128)(2,1)S(1)}, u32[]{:S(2)}, u32[]{:S(2)}) %collective-permute-start.2) | collective-permute-done | bytes 131104 | tf_op jit(solution)/shard_map/ppermute | solution.py:15
  174.5 5.2 %collective-permute-done.3 = bf16[2,512,64]{1,0,2:T(2,128)(2,1)S(1)} collective-permute-done((bf16[2,512,64]{1,0,2:T(2,128)(2,1)S(1)}, bf16[2,512,64]{1,0,2:T(2,128)(2,1)S(1)}, u32[]{:S(2)}, u32[]{:S(2)}) %collective-permute-start.3) | collective-permute-done | bytes 131104 | tf_op jit(solution)/shard_map/ppermute | solution.py:15
  180.1 5.2 %collective-permute-done.4 = bf16[2,512,64]{1,0,2:T(2,128)(2,1)S(1)} collective-permute-done((bf16[2,512,64]{1,0,2:T(2,128)(2,1)S(1)}, bf16[2,512,64]{1,0,2:T(2,128)(2,1)S(1)}, u32[]{:S(2)}, u32[]{:S(2)}) %collective-permute-start.4) | collective-permute-done | bytes 131104 | tf_op jit(solution)/shard_map/ppermute | solution.py:15
  185.7 5.2 %collective-permute-done.5 = bf16[2,512,64]{1,0,2:T(2,128)(2,1)S(1)} collective-permute-done((bf16[2,512,64]{1,0,2:T(2,128)(2,1)S(1)}, bf16[2,512,64]{1,0,2:T(2,128)(2,1)S(1)}, u32[]{:S(2)}, u32[]{:S(2)}) %collective-permute-start.5) | collective-permute-done | bytes 131104 | tf_op jit(solution)/shard_map/ppermute | solution.py:15
  191.3 5.2 %collective-permute-done.6 = bf16[2,512,64]{1,0,2:T(2,128)(2,1)S(1)} collective-permute-done((bf16[2,512,64]{1,0,2:T(2,128)(2,1)S(1)}, bf16[2,512,64]{1,0,2:T(2,128)(2,1)S(1)}, u32[]{:S(2)}, u32[]{:S(2)}) %collective-permute-start.6) | collective-permute-done | bytes 131104 | tf_op jit(solution)/shard_map/ppermute | solution.py:15
  196.9 5.2 %collective-permute-done.7 = bf16[2,512,64]{1,0,2:T(2,128)(2,1)S(1)} collective-permute-done((bf16[2,512,64]{1,0,2:T(2,128)(2,1)S(1)}, bf16[2,512,64]{1,0,2:T(2,128)(2,1)S(1)}, u32[]{:S(2)}, u32[]{:S(2)}) %collective-permute-start.7) | collective-permute-done | bytes 131104 | tf_op jit(solution)/shard_map/ppermute | solution.py:15
  202.5 5.2 %collective-permute-done.8 = bf16[2,512,64]{1,0,2:T(2,128)(2,1)S(1)} collective-permute-done((bf16[2,512,64]{1,0,2:T(2,128)(2,1)S(1)}, bf16[2,512,64]{1,0,2:T(2,128)(2,1)S(1)}, u32[]{:S(2)}, u32[]{:S(2)}) %collective-permute-start.8) | collective-permute-done | bytes 131104 | tf_op jit(solution)/shard_map/ppermute | solution.py:15
  208.1 5.2 %collective-permute-done.9 = bf16[2,512,64]{1,0,2:T(2,128)(2,1)S(1)} collective-permute-done((bf16[2,512,64]{1,0,2:T(2,128)(2,1)S(1)}, bf16[2,512,64]{1,0,2:T(2,128)(2,1)S(1)}, u32[]{:S(2)}, u32[]{:S(2)}) %collective-permute-start.9) | collective-permute-done | bytes 131104 | tf_op jit(solution)/shard_map/ppermute | solution.py:15
  213.7 5.2 %collective-permute-done.10 = bf16[2,512,64]{1,0,2:T(2,128)(2,1)S(1)} collective-permute-done((bf16[2,512,64]{1,0,2:T(2,128)(2,1)S(1)}, bf16[2,512,64]{1,0,2:T(2,128)(2,1)S(1)}, u32[]{:S(2)}, u32[]{:S(2)}) %collective-permute-start.10) | collective-permute-done | bytes 131104 | tf_op jit(solution)/shard_map/ppermute | solution.py:15
  219.3 5.2 %collective-permute-done.11 = bf16[2,512,64]{1,0,2:T(2,128)(2,1)S(1)} collective-permute-done((bf16[2,512,64]{1,0,2:T(2,128)(2,1)S(1)}, bf16[2,512,64]{1,0,2:T(2,128)(2,1)S(1)}, u32[]{:S(2)}, u32[]{:S(2)}) %collective-permute-start.11) | collective-permute-done | bytes 131104 | tf_op jit(solution)/shard_map/ppermute | solution.py:15
  224.9 5.2 %collective-permute-done.12 = bf16[2,512,64]{1,0,2:T(2,128)(2,1)S(1)} collective-permute-done((bf16[2,512,64]{1,0,2:T(2,128)(2,1)S(1)}, bf16[2,512,64]{1,0,2:T(2,128)(2,1)S(1)}, u32[]{:S(2)}, u32[]{:S(2)}) %collective-permute-start.12) | collective-permute-done | bytes 131104 | tf_op jit(solution)/shard_map/ppermute | solution.py:15
  230.5 5.2 %collective-permute-done.13 = bf16[2,512,64]{1,0,2:T(2,128)(2,1)S(1)} collective-permute-done((bf16[2,512,64]{1,0,2:T(2,128)(2,1)S(1)}, bf16[2,512,64]{1,0,2:T(2,128)(2,1)S(1)}, u32[]{:S(2)}, u32[]{:S(2)}) %collective-permute-start.13) | collective-permute-done | bytes 131104 | tf_op jit(solution)/shard_map/ppermute | solution.py:15
  236.1 5.2 %collective-permute-done.14 = bf16[2,512,64]{1,0,2:T(2,128)(2,1)S(1)} collective-permute-done((bf16[2,512,64]{1,0,2:T(2,128)(2,1)S(1)}, bf16[2,512,64]{1,0,2:T(2,128)(2,1)S(1)}, u32[]{:S(2)}, u32[]{:S(2)}) %collective-permute-start.14) | collective-permute-done | bytes 131104 | tf_op jit(solution)/shard_map/ppermute | solution.py:15
  241.8 2.0 fusion.2
  243.7 7.3 %all-to-all-start = ((bf16[16,32,512]{2,1,0:T(8,128)(2,1)}), bf16[16,32,512]{2,1,0:T(8,128)(2,1)S(1)}, u32[]{:S(2)}, u32[]{:S(2)}) async-start(bf16[16,32,512]{2,1,0:T(8,128)(2,1)} %bitcast.19), calls=%async_computation.1 | async-start | bytes 1048576 | tf_op jit(solution)/shard_map/all_to_all | solution.py:66
  251.1 12.2 %all-to-all-done = bf16[16,32,512]{2,1,0:T(8,128)(2,1)S(1)} async-done(((bf16[16,32,512]{2,1,0:T(8,128)(2,1)}), bf16[16,32,512]{2,1,0:T(8,128)(2,1)S(1)}, u32[]{:S(2)}, u32[]{:S(2)}) %all-to-all-start) | async-done | bytes 524320 | tf_op jit(solution)/shard_map/all_to_all | solution.py:66
  263.5 63.7 %reduce-scatter.2.cloned.1.call-done = bf16[32,8192]{1,0:T(8,128)(2,1)} async-done(((bf16[512,8192]{1,0:T(8,128)(2,1)}), bf16[32,8192]{1,0:T(8,128)(2,1)}) %reduce-scatter.2.cloned.1.call-update) | async-done | bytes 524304 | tf_op jit(solution)/shard_map/reduce_scatter | solution.py:35
  327.2 2.0 multiply_convert_fusion
  (56 shorter events, 10.2 us)
Async XLA Ops:
  6.5 52.2 %copy-start = (bf16[512,896]{1,0:T(8,128)(2,1)S(1)}, bf16[512,896]{1,0:T(8,128)(2,1)}, u32[]{:S(2)}) copy-start(bf16[512,896]{1,0:T(8,128)(2,1)} %param.6) | copy-start | bytes 2752516
  6.5 47.2 %all-gather.5.cloned.1.call-start = ((), (), s32[]{:S(2)}) async-start(), calls=%async_computation.4 | async-start | bytes 3899392 | tf_op jit(solution)/shard_map/all_gather | solution.py:38
  7.3 132.5 %all-gather.3.cloned.1.call-start = ((), (), s32[]{:S(2)}) async-start(), calls=%async_computation.2 | async-start | bytes 15597568 | tf_op jit(solution)/shard_map/all_gather | solution.py:32
  8.0 233.7 %all-reduce.2.cloned.1.call-start = ((), (), s32[]{:S(2)}) async-start(), calls=%async_computation.5 | async-start | bytes 131072 | tf_op jit(solution)/shard_map/psum | solution.py:56
  59.9 267.3 %reduce-scatter.2.cloned.1.call-start = ((), (), s32[]{:S(2)}) async-start(), calls=%async_computation.3 | async-start | bytes 8912896 | tf_op jit(solution)/shard_map/reduce_scatter | solution.py:35
  156.2 0.9 copy-start.1
  156.2 1.4 copy-start.2
  157.3 5.6 %collective-permute-start = (bf16[2,512,64]{1,0,2:T(2,128)(2,1)S(1)}, bf16[2,512,64]{1,0,2:T(2,128)(2,1)S(1)}, u32[]{:S(2)}, u32[]{:S(2)}) collective-permute-start(bf16[2,512,64]{1,0,2:T(2,128)(2,1)S(1)} %copy.12), channel_id=1, source_target_pairs={{0,16},{16,32},{32,48},{48,64},{64,80},{80,96},{96,112},{112,128},... | collective-permute-start | bytes 393224 | tf_op jit(solution)/shard_map/ppermute | solution.py:15
  162.9 5.6 %collective-permute-start.1 = (bf16[2,512,64]{1,0,2:T(2,128)(2,1)S(1)}, bf16[2,512,64]{1,0,2:T(2,128)(2,1)S(1)}, u32[]{:S(2)}, u32[]{:S(2)}) collective-permute-start(bf16[2,512,64]{1,0,2:T(2,128)(2,1)S(1)} %collective-permute-done), channel_id=1, source_target_pairs={{0,16},{16,32},{32,48},{48,64},{64,80},{80,96},{96,112},{112,128},... | collective-permute-start | bytes 393224 | tf_op jit(solution)/shard_map/ppermute | solution.py:15
  168.5 5.6 %collective-permute-start.2 = (bf16[2,512,64]{1,0,2:T(2,128)(2,1)S(1)}, bf16[2,512,64]{1,0,2:T(2,128)(2,1)S(1)}, u32[]{:S(2)}, u32[]{:S(2)}) collective-permute-start(bf16[2,512,64]{1,0,2:T(2,128)(2,1)S(1)} %collective-permute-done.1), channel_id=1, source_target_pairs={{0,16},{16,32},{32,48},{48,64},{64,80},{80,96},{96,112},{112,128},... | collective-permute-start | bytes 393224 | tf_op jit(solution)/shard_map/ppermute | solution.py:15
  168.9 82.2 %copy-start.3 = (s32[4]{0:T(128)S(1)}, s32[4]{0:T(128)}, u32[]{:S(2)}) copy-start(s32[4]{0:T(128)} %param.11) | copy-start | bytes 52
  174.1 5.6 %collective-permute-start.3 = (bf16[2,512,64]{1,0,2:T(2,128)(2,1)S(1)}, bf16[2,512,64]{1,0,2:T(2,128)(2,1)S(1)}, u32[]{:S(2)}, u32[]{:S(2)}) collective-permute-start(bf16[2,512,64]{1,0,2:T(2,128)(2,1)S(1)} %collective-permute-done.2), channel_id=1, source_target_pairs={{0,16},{16,32},{32,48},{48,64},{64,80},{80,96},{96,112},{112,128},... | collective-permute-start | bytes 393224 | tf_op jit(solution)/shard_map/ppermute | solution.py:15
  179.7 5.6 %collective-permute-start.4 = (bf16[2,512,64]{1,0,2:T(2,128)(2,1)S(1)}, bf16[2,512,64]{1,0,2:T(2,128)(2,1)S(1)}, u32[]{:S(2)}, u32[]{:S(2)}) collective-permute-start(bf16[2,512,64]{1,0,2:T(2,128)(2,1)S(1)} %collective-permute-done.3), channel_id=1, source_target_pairs={{0,16},{16,32},{32,48},{48,64},{64,80},{80,96},{96,112},{112,128},... | collective-permute-start | bytes 393224 | tf_op jit(solution)/shard_map/ppermute | solution.py:15
  185.3 5.6 %collective-permute-start.5 = (bf16[2,512,64]{1,0,2:T(2,128)(2,1)S(1)}, bf16[2,512,64]{1,0,2:T(2,128)(2,1)S(1)}, u32[]{:S(2)}, u32[]{:S(2)}) collective-permute-start(bf16[2,512,64]{1,0,2:T(2,128)(2,1)S(1)} %collective-permute-done.4), channel_id=1, source_target_pairs={{0,16},{16,32},{32,48},{48,64},{64,80},{80,96},{96,112},{112,128},... | collective-permute-start | bytes 393224 | tf_op jit(solution)/shard_map/ppermute | solution.py:15
  190.9 5.6 %collective-permute-start.6 = (bf16[2,512,64]{1,0,2:T(2,128)(2,1)S(1)}, bf16[2,512,64]{1,0,2:T(2,128)(2,1)S(1)}, u32[]{:S(2)}, u32[]{:S(2)}) collective-permute-start(bf16[2,512,64]{1,0,2:T(2,128)(2,1)S(1)} %collective-permute-done.5), channel_id=1, source_target_pairs={{0,16},{16,32},{32,48},{48,64},{64,80},{80,96},{96,112},{112,128},... | collective-permute-start | bytes 393224 | tf_op jit(solution)/shard_map/ppermute | solution.py:15
  196.5 5.6 %collective-permute-start.7 = (bf16[2,512,64]{1,0,2:T(2,128)(2,1)S(1)}, bf16[2,512,64]{1,0,2:T(2,128)(2,1)S(1)}, u32[]{:S(2)}, u32[]{:S(2)}) collective-permute-start(bf16[2,512,64]{1,0,2:T(2,128)(2,1)S(1)} %collective-permute-done.6), channel_id=1, source_target_pairs={{0,16},{16,32},{32,48},{48,64},{64,80},{80,96},{96,112},{112,128},... | collective-permute-start | bytes 393224 | tf_op jit(solution)/shard_map/ppermute | solution.py:15
  202.1 5.6 %collective-permute-start.8 = (bf16[2,512,64]{1,0,2:T(2,128)(2,1)S(1)}, bf16[2,512,64]{1,0,2:T(2,128)(2,1)S(1)}, u32[]{:S(2)}, u32[]{:S(2)}) collective-permute-start(bf16[2,512,64]{1,0,2:T(2,128)(2,1)S(1)} %collective-permute-done.7), channel_id=1, source_target_pairs={{0,16},{16,32},{32,48},{48,64},{64,80},{80,96},{96,112},{112,128},... | collective-permute-start | bytes 393224 | tf_op jit(solution)/shard_map/ppermute | solution.py:15
  207.7 5.6 %collective-permute-start.9 = (bf16[2,512,64]{1,0,2:T(2,128)(2,1)S(1)}, bf16[2,512,64]{1,0,2:T(2,128)(2,1)S(1)}, u32[]{:S(2)}, u32[]{:S(2)}) collective-permute-start(bf16[2,512,64]{1,0,2:T(2,128)(2,1)S(1)} %collective-permute-done.8), channel_id=1, source_target_pairs={{0,16},{16,32},{32,48},{48,64},{64,80},{80,96},{96,112},{112,128},... | collective-permute-start | bytes 393224 | tf_op jit(solution)/shard_map/ppermute | solution.py:15
  213.3 5.6 %collective-permute-start.10 = (bf16[2,512,64]{1,0,2:T(2,128)(2,1)S(1)}, bf16[2,512,64]{1,0,2:T(2,128)(2,1)S(1)}, u32[]{:S(2)}, u32[]{:S(2)}) collective-permute-start(bf16[2,512,64]{1,0,2:T(2,128)(2,1)S(1)} %collective-permute-done.9), channel_id=1, source_target_pairs={{0,16},{16,32},{32,48},{48,64},{64,80},{80,96},{96,112},{112,128},... | collective-permute-start | bytes 393224 | tf_op jit(solution)/shard_map/ppermute | solution.py:15
  218.9 5.6 %collective-permute-start.11 = (bf16[2,512,64]{1,0,2:T(2,128)(2,1)S(1)}, bf16[2,512,64]{1,0,2:T(2,128)(2,1)S(1)}, u32[]{:S(2)}, u32[]{:S(2)}) collective-permute-start(bf16[2,512,64]{1,0,2:T(2,128)(2,1)S(1)} %collective-permute-done.10), channel_id=1, source_target_pairs={{0,16},{16,32},{32,48},{48,64},{64,80},{80,96},{96,112},{112,128},... | collective-permute-start | bytes 393224 | tf_op jit(solution)/shard_map/ppermute | solution.py:15
  224.5 5.6 %collective-permute-start.12 = (bf16[2,512,64]{1,0,2:T(2,128)(2,1)S(1)}, bf16[2,512,64]{1,0,2:T(2,128)(2,1)S(1)}, u32[]{:S(2)}, u32[]{:S(2)}) collective-permute-start(bf16[2,512,64]{1,0,2:T(2,128)(2,1)S(1)} %collective-permute-done.11), channel_id=1, source_target_pairs={{0,16},{16,32},{32,48},{48,64},{64,80},{80,96},{96,112},{112,128},... | collective-permute-start | bytes 393224 | tf_op jit(solution)/shard_map/ppermute | solution.py:15
  230.2 5.6 %collective-permute-start.13 = (bf16[2,512,64]{1,0,2:T(2,128)(2,1)S(1)}, bf16[2,512,64]{1,0,2:T(2,128)(2,1)S(1)}, u32[]{:S(2)}, u32[]{:S(2)}) collective-permute-start(bf16[2,512,64]{1,0,2:T(2,128)(2,1)S(1)} %collective-permute-done.12), channel_id=1, source_target_pairs={{0,16},{16,32},{32,48},{48,64},{64,80},{80,96},{96,112},{112,128},... | collective-permute-start | bytes 393224 | tf_op jit(solution)/shard_map/ppermute | solution.py:15
  235.8 5.6 %collective-permute-start.14 = (bf16[2,512,64]{1,0,2:T(2,128)(2,1)S(1)}, bf16[2,512,64]{1,0,2:T(2,128)(2,1)S(1)}, u32[]{:S(2)}, u32[]{:S(2)}) collective-permute-start(bf16[2,512,64]{1,0,2:T(2,128)(2,1)S(1)} %collective-permute-done.13), channel_id=1, source_target_pairs={{0,16},{16,32},{32,48},{48,64},{64,80},{80,96},{96,112},{112,128},... | collective-permute-start | bytes 393224 | tf_op jit(solution)/shard_map/ppermute | solution.py:15
  243.7 19.6 %all-to-all-start = ((bf16[16,32,512]{2,1,0:T(8,128)(2,1)}), bf16[16,32,512]{2,1,0:T(8,128)(2,1)S(1)}, u32[]{:S(2)}, u32[]{:S(2)}) async-start(bf16[16,32,512]{2,1,0:T(8,128)(2,1)} %bitcast.19), calls=%async_computation.1 | async-start | bytes 1048576 | tf_op jit(solution)/shard_map/all_to_all | solution.py:66
Sparse Core Ops, SparseCore 0:
  9.2 44.5 all-gather.4
  55.6 84.1 all-gather.2
  143.0 89.2 all-reduce.1
  236.3 90.8 reduce-scatter.1
